TPU v7x, 32 devices: a whole 2x2x4 slice. The times are simulated.
32 devices in a mesh: vec: 8 (over y, x, core), fld: 4 (over z).
Axes of the slice: x: 2, y: 2, z: 4, core: 2. Of those that a mesh axis runs over, the one named last changes fastest.
Arguments:
- profiles: float32 [1024, 32768], P('vec', 'fld'), may hold values from 0.04 to 21
- pivots: int32 [8, 4], P('vec'), may hold values from 0 to 127
- roles: int32 [8, 3], P('vec'), may hold values from 0 to 2, each once within a row
Outputs:
- pair_means: float32 [8, 128, 3, 128], P('vec', 'fld')
- similarity: float32 [8, 128, 4, 128], P('vec', 'fld')
Inputs may be any that keep to these rules, and one draw needn't show every extreme that they name: Each row of roles holds 0, 1 and 2 once each.
All inputs are finite; a program needn't handle non-finite values.
Results may differ from a plain program's by a relative error of at most 0.0003.
Values sent between devices are 32-bit elements; how exact they have to be, the bound alone decides.
A program may use at most 128 MiB of HBM per device.

v0:
```python
import jax
import jax.numpy as jnp
from jax import lax
from jax.sharding import PartitionSpec as P

FIELDS = 32768


def shifted(shard, axis, by):
    peers = lax.axis_size(axis)
    return lax.ppermute(shard, axis, [(i, (i + by) % peers) for i in range(peers)])


def min_sums(left_rows, right_rows):
    total = left_rows.shape[0]
    group_size = 16 if total % 16 == 0 else total
    stacked = left_rows.reshape(total // group_size, group_size, left_rows.shape[1])

    def block_sum(part_rows):
        return jnp.sum(jnp.minimum(part_rows[:, None, :], right_rows[None, :, :]), axis=2)

    return lax.map(block_sum, stacked).reshape(total, right_rows.shape[0])


def body(profiles, pivots, roles):
    stride = lax.axis_size("vec") // 8
    width = profiles.shape[0]
    count_piv = pivots.shape[1]
    row_count = width // lax.axis_size("fld")
    field_scale = 1.0 / FIELDS
    near_block = shifted(profiles, "vec", stride)
    far_block = shifted(profiles, "vec", 2 * stride)
    blocks = jnp.stack([profiles, near_block, far_block])
    lead_block = blocks[roles[0, 0]]
    pivot_block = blocks[roles[0, 1]]
    tail_block = blocks[roles[0, 2]]
    chosen = pivots[0]
    pivot_vectors = pivot_block[chosen]
    crossed = jnp.minimum(pivot_vectors[:, None, :], tail_block[None, :, :]).reshape(
        count_piv * width, profiles.shape[1]
    )
    joined_right = jnp.concatenate([pivot_block, tail_block, crossed], 0)
    lead_part = min_sums(lead_block, joined_right)
    middle_part = min_sums(pivot_block, tail_block)
    tables = (
        lax.psum_scatter(
            jnp.concatenate(
                [
                    lead_part[:, : 2 * width].reshape(row_count * lax.axis_size("fld"), 2, width),
                    middle_part[:, None, :],
                    lead_part[:, 2 * width :].reshape(
                        row_count * lax.axis_size("fld"), count_piv, width
                    ),
                ],
                1,
            ),
            "fld",
            scatter_dimension=0,
            tiled=True,
        )
        * field_scale
    )
    pair_tables = tables[:, :3, :]
    triple = tables[:, 3:, :]
    pivot_part = min_sums(pivot_vectors, tail_block)
    pivot_rows = lax.psum(pivot_part, "fld") * field_scale
    first_cols = jnp.take(pair_tables[:, 0, :], chosen, axis=1)
    similar = (
        first_cols[:, :, None] + pair_tables[:, 1, :][:, None, :] + pivot_rows[None, :, :] - triple
    ) * 0.5
    return (pair_tables[None], similar[None])


def solution(mesh):
    return jax.shard_map(
        body,
        mesh=mesh,
        in_specs=(P("vec", "fld"), P("vec", None), P("vec", None)),
        out_specs=(P("vec", "fld", None, None), P("vec", "fld", None, None)),
        check_vma=False,
    )
```

profile of v0, /device:TPU:1, one launch (start us, length us, event | category | flops | bytes accessed | tf_op | source)
XLA Modules:
  0.0 803.8 jit_solution(6472845069573763283)
XLA Ops:
  18.8 81.1 %collective-permute-done = f32[128,8192]{1,0:T(8,128)} collective-permute-done((f32[128,8192]{1,0:T(8,128)}, f32[128,8192]{1,0:T(8,128)}, u32[]{:S(2)}, u32[]{:S(2)}) %collective-permute-start) | collective-permute-done | bytes 4194336 | tf_op jit(solution)/shard_map/ppermute | solution.py:11
  99.9 46.4 %collective-permute-done.1 = f32[128,8192]{1,0:T(8,128)} collective-permute-done((f32[128,8192]{1,0:T(8,128)}, f32[128,8192]{1,0:T(8,128)}, u32[]{:S(2)}, u32[]{:S(2)}) %collective-permute-start.1) | collective-permute-done | bytes 4194336 | tf_op jit(solution)/shard_map/ppermute | solution.py:11
  146.3 10.6 %pad_maximum_fusion.1 = f32[3,128,8192]{2,1,0:T(8,128)} fusion(f32[1,128,8192]{2,1,0:T(8,128)} %bitcast.7, f32[1,128,8192]{2,1,0:T(8,128)} %bitcast.6, f32[1,128,8192]{2,1,0:T(8,128)} %bitcast.58), kind=kLoop, calls=%fused_computation.9 | loop fusion | flops 6291456 | bytes 25165824 | tf_op jit(solution)/shard_map/stack | solution.py:33
  157.0 9.6 %constant_dynamic-slice_fusion.1 = (f32[1,128,8192]{2,1,0:T(8,128)}, f32[1,128,8192]{2,1,0:T(8,128)}, f32[1,128,8192]{2,1,0:T(8,128)}) fusion(f32[3,128,8192]{2,1,0:T(8,128)} %pad_maximum_fusion.1, s32[]{:T(128)S(6)} %select_n.35, s32[]{:T(128)S(6)} %select_n.36, s32[]{:T(128)S(6)} %select_n.34), kind=kLoop, calls=%fused_computation.27 | loop fusion | bytes 25165836 | tf_op jit(solution)/shard_map/dynamic_slice | solution.py:35
  169.5 10.5 %fusion = (f32[4,128]{1,0:T(4,128)S(1)}, f32[4,128,8192]{2,1,0:T(8,128)}) fusion(f32[128,8192]{1,0:T(8,128)} %bitcast.50, f32[4,8192]{1,0:T(4,128)S(1)} %gather_fusion), kind=kLoop, calls=%fused_computation.11 | loop fusion | flops 8388096 | bytes 21104640 | tf_op jit(solution)/shard_map/while/body/eval_jaxpr/reduce_sum | solution.py:20
  179.9 15.6 %pad_maximum_fusion = f32[768,8192]{1,0:T(8,128)} fusion(f32[512,8192]{1,0:T(8,128)} %bitcast.53, f32[128,8192]{1,0:T(8,128)S(1)} %bitcast.51, f32[128,8192]{1,0:T(8,128)} %bitcast.55), kind=kLoop, calls=%fused_computation.8 | loop fusion | flops 12582912 | bytes 50331648 | tf_op jit(solution)/shard_map/concatenate | solution.py:42
  195.6 510.4 %while.24 = (s32[]{:T(128)}, f32[8,16,768]{2,1,0:T(8,128)S(1)}, f32[8,16,8192]{2,1,0:T(8,128)}, f32[768,8192]{1,0:T(8,128)}, s32[]{:T(128)}) while((s32[]{:T(128)}, f32[8,16,768]{2,1,0:T(8,128)S(1)}, f32[8,16,8192]{2,1,0:T(8,128)}, f32[768,8192]{1,0:T(8,128)}, s32[]{:T(128)}) %tuple.56), condition=%wide.region_2.3_spmd, body=%wide.region_0.2_spmd.sunk | while | flops 201314304 | bytes 26886212 | solution.py:22
  196.6 62.7 %minimum_reduce_fusion.4 = f32[16,768]{1,0:T(8,128)S(1)} fusion(f32[768,8192]{1,0:T(8,128)} %get-tuple-element.157, f32[16,8192]{1,0:T(8,128)S(1)} %dynamic-slice_bitcast_fusion.4), kind=kLoop, calls=%fused_computation.2.clone.1 | loop fusion | flops 201314304 | bytes 25739264 | tf_op jit(solution)/shard_map/while/body/eval_jaxpr/reduce_sum | solution.py:20
  260.4 62.7 %minimum_reduce_fusion.4 = f32[16,768]{1,0:T(8,128)S(1)} fusion(f32[768,8192]{1,0:T(8,128)} %get-tuple-element.157, f32[16,8192]{1,0:T(8,128)S(1)} %dynamic-slice_bitcast_fusion.4), kind=kLoop, calls=%fused_computation.2.clone.1 | loop fusion | flops 201314304 | bytes 25739264 | tf_op jit(solution)/shard_map/while/body/eval_jaxpr/reduce_sum | solution.py:20
  324.3 62.7 %minimum_reduce_fusion.4 = f32[16,768]{1,0:T(8,128)S(1)} fusion(f32[768,8192]{1,0:T(8,128)} %get-tuple-element.157, f32[16,8192]{1,0:T(8,128)S(1)} %dynamic-slice_bitcast_fusion.4), kind=kLoop, calls=%fused_computation.2.clone.1 | loop fusion | flops 201314304 | bytes 25739264 | tf_op jit(solution)/shard_map/while/body/eval_jaxpr/reduce_sum | solution.py:20
  388.1 62.7 %minimum_reduce_fusion.4 = f32[16,768]{1,0:T(8,128)S(1)} fusion(f32[768,8192]{1,0:T(8,128)} %get-tuple-element.157, f32[16,8192]{1,0:T(8,128)S(1)} %dynamic-slice_bitcast_fusion.4), kind=kLoop, calls=%fused_computation.2.clone.1 | loop fusion | flops 201314304 | bytes 25739264 | tf_op jit(solution)/shard_map/while/body/eval_jaxpr/reduce_sum | solution.py:20
  451.9 62.7 %minimum_reduce_fusion.4 = f32[16,768]{1,0:T(8,128)S(1)} fusion(f32[768,8192]{1,0:T(8,128)} %get-tuple-element.157, f32[16,8192]{1,0:T(8,128)S(1)} %dynamic-slice_bitcast_fusion.4), kind=kLoop, calls=%fused_computation.2.clone.1 | loop fusion | flops 201314304 | bytes 25739264 | tf_op jit(solution)/shard_map/while/body/eval_jaxpr/reduce_sum | solution.py:20
  515.7 62.7 %minimum_reduce_fusion.4 = f32[16,768]{1,0:T(8,128)S(1)} fusion(f32[768,8192]{1,0:T(8,128)} %get-tuple-element.157, f32[16,8192]{1,0:T(8,128)S(1)} %dynamic-slice_bitcast_fusion.4), kind=kLoop, calls=%fused_computation.2.clone.1 | loop fusion | flops 201314304 | bytes 25739264 | tf_op jit(solution)/shard_map/while/body/eval_jaxpr/reduce_sum | solution.py:20
  579.5 62.7 %minimum_reduce_fusion.4 = f32[16,768]{1,0:T(8,128)S(1)} fusion(f32[768,8192]{1,0:T(8,128)} %get-tuple-element.157, f32[16,8192]{1,0:T(8,128)S(1)} %dynamic-slice_bitcast_fusion.4), kind=kLoop, calls=%fused_computation.2.clone.1 | loop fusion | flops 201314304 | bytes 25739264 | tf_op jit(solution)/shard_map/while/body/eval_jaxpr/reduce_sum | solution.py:20
  643.3 62.7 %minimum_reduce_fusion.4 = f32[16,768]{1,0:T(8,128)S(1)} fusion(f32[768,8192]{1,0:T(8,128)} %get-tuple-element.157, f32[16,8192]{1,0:T(8,128)S(1)} %dynamic-slice_bitcast_fusion.4), kind=kLoop, calls=%fused_computation.2.clone.1 | loop fusion | flops 201314304 | bytes 25739264 | tf_op jit(solution)/shard_map/while/body/eval_jaxpr/reduce_sum | solution.py:20
  706.2 65.3 %while.25 = (s32[]{:T(128)}, f32[8,16,128]{2,1,0:T(8,128)S(1)}, f32[8,16,8192]{2,1,0:T(8,128)}, f32[1,128,8192]{2,1,0:T(8,128)}, s32[]{:T(128)}) while((s32[]{:T(128)}, f32[8,16,128]{2,1,0:T(8,128)S(1)}, f32[8,16,8192]{2,1,0:T(8,128)}, f32[1,128,8192]{2,1,0:T(8,128)}, s32[]{:T(128)}) %tuple.55), condition=%wide.region_5.6_spmd, body=%wide.region_3.5_spmd.sunk | while | flops 33552384 | bytes 5791813 | solution.py:22
  707.3 7.0 minimum_reduce_fusion.5
  715.5 7.0 minimum_reduce_fusion.5
  723.7 7.0 minimum_reduce_fusion.5
  731.8 7.0 minimum_reduce_fusion.5
  740.0 7.0 minimum_reduce_fusion.5
  748.2 7.0 minimum_reduce_fusion.5
  772.6 10.8 %psum.7 = f32[4,128]{1,0:T(4,128)S(1)} all-reduce(f32[4,128]{1,0:T(4,128)S(1)} %get-tuple-element.87), channel_id=1, replica_groups=mesh['vec'=8,'fld'=4] {'fld'}, use_global_device_ids=true, to_apply=%region_8.9 | all-reduce | flops 512 | bytes 4096 | tf_op jit(solution)/shard_map/psum | solution.py:66
  783.4 10.1 %reduce-scatter.2.cloned.1.call-done = f32[32,7,128]{2,1,0:T(8,128)} async-done(((f32[128,7,128]{2,1,0:T(8,128)}), f32[32,7,128]{2,1,0:T(8,128)}) %reduce-scatter.2.cloned.1.call-update) | async-done | bytes 114704 | tf_op jit(solution)/shard_map/reduce_scatter | solution.py:46
  (64 shorter events, 44.9 us)
Async XLA Ops:
  7.2 786.3 %reduce-scatter.2.cloned.1.call-start = ((), (), s32[]{:S(2)}) async-start(), calls=%async_computation.1 | async-start | bytes 655360 | tf_op jit(solution)/shard_map/reduce_scatter | solution.py:46
  7.2 92.7 %collective-permute-start = (f32[128,8192]{1,0:T(8,128)}, f32[128,8192]{1,0:T(8,128)}, u32[]{:S(2)}, u32[]{:S(2)}) collective-permute-start(f32[128,8192]{1,0:T(8,128)} %param.7), channel_id=1, source_target_pairs={{0,4},{4,8},{8,12},{12,16},{16,20},{20,24},{24,28},{28,0},{1,5},{5... | collective-permute-start | bytes 12582920 | tf_op jit(solution)/shard_map/ppermute | solution.py:11
  9.9 136.5 %collective-permute-start.1 = (f32[128,8192]{1,0:T(8,128)}, f32[128,8192]{1,0:T(8,128)}, u32[]{:S(2)}, u32[]{:S(2)}) collective-permute-start(f32[128,8192]{1,0:T(8,128)} %param.7), channel_id=1, source_target_pairs={{0,8},{4,12},{8,16},{12,20},{16,24},{20,28},{24,0},{28,4},{1,9},{5... | collective-permute-start | bytes 12582920 | tf_op jit(solution)/shard_map/ppermute | solution.py:11
  169.5 10.5 %copy-start = (f32[1,128,8192]{2,1,0:T(8,128)S(1)}, f32[1,128,8192]{2,1,0:T(8,128)}, u32[]{:S(2)}) copy-start(f32[1,128,8192]{2,1,0:T(8,128)} %get-tuple-element.162) | copy-start | bytes 12582916
  706.2 66.4 %copy-start.1 = (s32[1,4]{1,0:T(1,128)S(1)}, s32[1,4]{1,0:T(1,128)}, u32[]{:S(2)}) copy-start(s32[1,4]{1,0:T(1,128)} %param.8) | copy-start | bytes 52
Sparse Core Ops, SparseCore 0:
  772.7 20.7 reduce-scatter.1
where the time goes:
time: 807 us; the launch traced here: 804 us
  other arithmetic  596 us (74%)
  waiting for transfers between devices  138 us (17%)
  local copies, waits for them, and re-layouts  34.6 us (4%)
  between operations  19.9 us (2%)
  blocking collectives  10.8 us (1%)
    reduce_sum x17, other arithmetic, block_sum(): jnp.sum(jnp.minimum(part_rows[:, None, :], right_rows[None, :, :]), axis=2)  568 us
    ppermute x2, waiting for transfers between devices, shifted(): lax.ppermute(shard, axis, [(i, (i + by) % peers) for i in range(peers)])  128 us
    min x16, local copies, waits for them, and re-layouts, block_sum(): jnp.minimum(part_rows[:, None, :], right_rows[None, :, :])  17.3 us
  transfers between devices with their start and end apart: 3, of which 3 were waited for; matrix products, arithmetic and copies ran while one was open for 0% of the time, Pallas kernels for 0%

commit v1 on v0

v1 whole, which is shorter than its diff:
```python
import functools

import jax
import jax.numpy as jnp
from jax import lax
from jax.experimental import pallas as pl
from jax.experimental.pallas import tpu as pltpu
from jax.sharding import PartitionSpec as P

FIELDS = 32768
CHUNKS = 2
LANES = 128
SUB = 8


def shifted(shard, axis, by):
    peers = lax.axis_size(axis)
    return lax.ppermute(shard, axis, [(i, (i + by) % peers) for i in range(peers)])


def table_kernel(unroll, roles, pivots, own, near, far, out, held, piv, sems):
    rows, width = own.shape
    count = piv.shape[0]
    steps = width // LANES
    copies = [
        pltpu.make_async_copy(block, held.at[i], sems.at[i])
        for i, block in enumerate((own, near, far))
    ]
    for copy in copies:
        copy.start()
    for copy in copies:
        copy.wait()
    first, middle, last = roles[0], roles[1], roles[2]

    def tile(which, row, col):
        return held[which, pl.ds(pl.multiple_of(row, SUB), SUB), pl.ds(pl.multiple_of(col, LANES), LANES)]

    sub_id = lax.broadcasted_iota(jnp.int32, (SUB, LANES), 0)
    lane_id = lax.broadcasted_iota(jnp.int32, (SUB, LANES), 1)
    for m in range(count):
        base = (pivots[m] // SUB) * SUB
        keep = sub_id == pivots[m] - base

        def spread(step, carry, m=m, base=base, keep=keep):
            col = step * LANES
            value = jnp.sum(jnp.where(keep, tile(middle, base, col), 0.0), axis=0, keepdims=True)
            piv[m, :, pl.ds(pl.multiple_of(col, LANES), LANES)] = jnp.broadcast_to(value, (SUB, LANES))
            return carry

        lax.fori_loop(0, steps, spread, 0)

    def store(table, row, col, sums):
        where = pl.ds(pl.multiple_of(row, SUB), SUB)
        current = out[table, where, :]
        for j, acc in enumerate(sums):
            total = jnp.sum(acc, axis=1, keepdims=True)
            current = jnp.where(lane_id == col + j, total, current)
        out[table, where, :] = current

    def triple_block(index, carry):
        row = (index // (rows // SUB)) * SUB
        col = (index % (rows // SUB)) * SUB

        def step(k, accs):
            at = k * LANES
            lead = tile(first, row, at)
            tail = tile(last, col, at)
            points = [piv[m, :, pl.ds(pl.multiple_of(at, LANES), LANES)] for m in range(count)]
            new = []
            for j in range(SUB):
                both = jnp.minimum(lead, jnp.broadcast_to(tail[j : j + 1], (SUB, LANES)))
                new.append(accs[j * (count + 1)] + both)
                for m in range(count):
                    new.append(accs[j * (count + 1) + 1 + m] + jnp.minimum(both, points[m]))
            return tuple(new)

        zero = jnp.zeros((SUB, LANES), jnp.float32)
        accs = lax.fori_loop(0, steps, step, (zero,) * (SUB * (count + 1)), unroll=unroll)
        store(1, row, col, accs[0 :: count + 1])
        for m in range(count):
            store(3 + m, row, col, accs[1 + m :: count + 1])
        return carry

    lax.fori_loop(0, (rows // SUB) ** 2, triple_block, 0)

    def pair_table(table, left, right):
        group = 4 if rows % (4 * SUB) == 0 else 1

        def pair_block(index, carry):
            row = (index // (rows // SUB)) * SUB * group
            col = (index % (rows // SUB)) * SUB

            def step(k, accs):
                at = k * LANES
                leads = [tile(left, row + g * SUB, at) for g in range(group)]
                tail = tile(right, col, at)
                new = []
                for j in range(SUB):
                    spread = jnp.broadcast_to(tail[j : j + 1], (SUB, LANES))
                    for g in range(group):
                        new.append(accs[j * group + g] + jnp.minimum(leads[g], spread))
                return tuple(new)

            zero = jnp.zeros((SUB, LANES), jnp.float32)
            accs = lax.fori_loop(0, steps, step, (zero,) * (SUB * group), unroll=unroll)
            for g in range(group):
                store(table, row + g * SUB, col, accs[g::group])
            return carry

        lax.fori_loop(0, (rows // SUB) * (rows // SUB // group), pair_block, 0)

    pair_table(0, first, middle)
    pair_table(2, middle, last)


def partial_tables(roles, pivots, own, near, far):
    rows, width = own.shape
    count = pivots.shape[0]
    smem = pl.BlockSpec(memory_space=pltpu.SMEM)
    hbm = pl.BlockSpec(memory_space=pl.ANY)
    pairs = (3 + count) * rows * rows * width
    return pl.pallas_call(
        functools.partial(table_kernel, 2),
        out_shape=jax.ShapeDtypeStruct((3 + count, rows, rows), jnp.float32),
        in_specs=[smem, smem, hbm, hbm, hbm],
        out_specs=pl.BlockSpec(memory_space=pltpu.VMEM),
        scratch_shapes=[
            pltpu.VMEM((3, rows, width), jnp.float32),
            pltpu.VMEM((count, SUB, width), jnp.float32),
            pltpu.SemaphoreType.DMA((3,)),
        ],
        compiler_params=pltpu.CompilerParams(vmem_limit_bytes=40 << 20),
        cost_estimate=pl.CostEstimate(
            flops=2 * pairs, bytes_accessed=3 * rows * width * 4, transcendentals=0
        ),
    )(roles, pivots, own, near, far)


def body(profiles, pivots, roles):
    stride = lax.axis_size("vec") // 8
    n = lax.axis_size("fld")
    width, fields = profiles.shape
    count_piv = pivots.shape[1]
    row_count = width // n
    chosen = pivots[0]
    chunks = CHUNKS if fields % (CHUNKS * LANES) == 0 else 1
    span = fields // chunks
    tables = None
    for k in range(chunks):
        own = profiles[:, k * span : (k + 1) * span]
        near = shifted(own, "vec", stride)
        far = shifted(own, "vec", 2 * stride)
        part = partial_tables(roles[0], chosen, own, near, far)
        tables = part if tables is None else tables + part

    pivot_part = jnp.take(tables[2], chosen, axis=0)
    me = lax.axis_index("fld")
    total = None
    for by in range(n):
        start = lax.rem(me + by, n) * row_count
        piece = lax.dynamic_slice_in_dim(tables, start, row_count, axis=1)
        piece = piece.reshape((3 + count_piv) * row_count, width)
        piece = jnp.concatenate([piece, pivot_part], 0)
        if by:
            piece = shifted(piece, "fld", by)
        total = piece if total is None else total + piece
    total = total * (1.0 / FIELDS)
    rows = total[: (3 + count_piv) * row_count].reshape(3 + count_piv, row_count, width)
    pivot_rows = total[(3 + count_piv) * row_count :]
    first_cols = jnp.take(rows[0], chosen, axis=1)
    pair_tables = jnp.transpose(rows[:3], (1, 0, 2))
    triple = jnp.transpose(rows[3:], (1, 0, 2))
    similar = (
        first_cols[:, :, None] + pair_tables[:, 1, :][:, None, :] + pivot_rows[None, :, :] - triple
    ) * 0.5
    return (pair_tables[None], similar[None])


def solution(mesh):
    return jax.shard_map(
        body,
        mesh=mesh,
        in_specs=(P("vec", "fld"), P("vec", None), P("vec", None)),
        out_specs=(P("vec", "fld", None, None), P("vec", "fld", None, None)),
        check_vma=False,
    )
```

time: 807 us -> 641 us (0.79)
  other arithmetic: 596 us -> 0.49 us
  Pallas kernels: 0 us -> 528 us
  waiting for transfers between devices: 138 us -> 94.4 us
  local copies, waits for them, and re-layouts: 34.6 us -> 6.72 us
  between operations: 19.9 us -> 0.81 us
  blocking collectives: 10.8 us -> 0 us
    reduce_sum x17 -> x0, other arithmetic: 568 us -> none  [block_sum(): jnp.sum(jnp.minimum(part_rows[:, None, :], right_rows[None, :, :]), axis=2)]
    pallas_call x0 -> x2, Pallas kernels: none -> 528 us  [partial_tables(): pl.pallas_call(functools.partial(table_kernel, 2), out_shape=jax.ShapeDty...]
    ppermute x2 -> x7, waiting for transfers between devices: 128 us -> 94.4 us  [shifted(): lax.ppermute(shard, axis, [(i, (i + by) % peers) for i in range(peers)])]
    min x16 -> x0, local copies, waits for them, and re-layouts: 17.3 us -> none  [block_sum(): jnp.minimum(part_rows[:, None, :], right_rows[None, :, :])]
    concatenate x2 -> x1, other arithmetic: 16.6 us -> 0.09 us  [body(): piece = jnp.concatenate([piece, pivot_part], 0)]
    psum x1 -> x0, blocking collectives: 10.8 us -> none  [body(): pivot_rows = lax.psum(pivot_part, 'fld') * field_scale]
    another operation x1 -> x0, other arithmetic: 10.6 us -> none  [body(): blocks = jnp.stack([profiles, near_block, far_block])]
    reduce_scatter x1 -> x0, waiting for transfers between devices: 10.1 us -> none  [body(): lax.psum_scatter(jnp.concatenate([lead_part[:, :2 * width].reshape(row_co...]
  transfers between devices with their start and end apart: 3 -> 7, of which waited for: 3 -> 4; matrix products, arithmetic and copies ran while one was open for 0% -> 0% of each run, Pallas kernels for 0% -> 41%
where the time goes in v1:
time: 641 us
  Pallas kernels  528 us (82%)
  waiting for transfers between devices  94.4 us (15%)
  starting transfers between devices  10.2 us (2%)
  local copies, waits for them, and re-layouts  6.72 us (1%)
    pallas_call x2, Pallas kernels, partial_tables(): pl.pallas_call(functools.partial(table_kernel, 2), out_shape=jax.ShapeDty...  528 us
    ppermute x7, waiting for transfers between devices, shifted(): lax.ppermute(shard, axis, [(i, (i + by) % peers) for i in range(peers)])  94.4 us
  transfers between devices with their start and end apart: 7, of which 4 were waited for; matrix products, arithmetic and copies ran while one was open for 0% of the time, Pallas kernels for 41%

profile of v1, /device:TPU:1, one launch (start us, length us, event | category | flops | bytes accessed | tf_op | source)
XLA Modules:
  0.0 640.8 jit_solution(14102404506996490887)
XLA Ops:
  0.6 3.9 fusion.5
  4.6 2.6 collective-permute-start
  7.2 1.2 collective-permute-start.1
  8.4 0.3 collective-permute-start.2
  8.7 1.2 collective-permute-start.3
  9.9 42.4 %collective-permute-done.near = f32[128,4096]{1,0:T(8,128)} collective-permute-done((f32[128,4096]{1,0:T(8,128)}, f32[128,4096]{1,0:T(8,128)}, u32[]{:S(2)}, u32[]{:S(2)}) %collective-permute-start) | collective-permute-done | bytes 2097184 | tf_op jit(solution)/shard_map/ppermute | solution.py:18
  52.4 45.8 %collective-permute-done.1.far = f32[128,4096]{1,0:T(8,128)} collective-permute-done((f32[128,4096]{1,0:T(8,128)}, f32[128,4096]{1,0:T(8,128)}, u32[]{:S(2)}, u32[]{:S(2)}) %collective-permute-start.1) | collective-permute-done | bytes 2097184 | tf_op jit(solution)/shard_map/ppermute | solution.py:18
  98.2 264.4 %shard_map.50 = f32[7,128,128]{2,1,0:T(8,128)S(1)} custom-call(s32[3]{0:T(128)S(1)} %bitcast.27, s32[4]{0:T(128)S(1)} %bitcast.29, f32[128,4096]{1,0:T(8,128)} %get-tuple-element.5.own, f32[128,4096]{1,0:T(8,128)} %collective-permute-done.near, f32[128,4096]{1,0:T(8,128)} %collective-permute-done.1.far), custom_call_target="tpu_custom_call" | custom-call | flops 939524096 | bytes 6291456 | tf_op jit(solution)/shard_map/pallas_call | solution.py:122
  362.6 263.9 %shard_map.51 = f32[7,128,128]{2,1,0:T(8,128)S(1)} custom-call(s32[3]{0:T(128)S(1)} %bitcast.28, s32[4]{0:T(128)S(1)} %bitcast.30, f32[128,4096]{1,0:T(8,128)S(1)} %get-tuple-element.4.own, f32[128,4096]{1,0:T(8,128)} %collective-permute-done.2.near, f32[128,4096]{1,0:T(8,128)} %collective-permute-done.3.far), custom_call_target="tpu_custom_call" | custom-call | flops 939524096 | bytes 6291456 | tf_op jit(solution)/shard_map/pallas_call | solution.py:122
  626.5 0.6 gather_fusion
  627.2 0.1 copy.14
  627.3 0.1 copy.15
  627.4 0.1 copy.17
  627.5 0.1 copy.19
  627.6 0.1 pad_maximum_fusion.2
  627.7 4.4 collective-permute-start.6
  632.1 0.5 collective-permute-start.4
  632.6 0.1 copy.13
  632.7 1.4 collective-permute-done.6
  634.1 4.8 collective-permute-done.5
  638.9 0.1 fusion.3
  639.3 0.1 copy.23
  639.4 0.6 gather_fusion.1
  640.2 0.7 copy.24
  (26 shorter events, 0.7 us)
Async XLA Ops:
  0.6 9.3 %copy-start.1 = (s32[1,4]{1,0:T(1,128)S(1)}, s32[1,4]{1,0:T(1,128)}, u32[]{:S(2)}) copy-start(s32[1,4]{1,0:T(1,128)} %param.4) | copy-start | bytes 52
  0.6 97.5 %copy-start = (s32[1,3]{1,0:T(1,128)S(1)}, s32[1,3]{1,0:T(1,128)}, u32[]{:S(2)}) copy-start(s32[1,3]{1,0:T(1,128)} %param.5) | copy-start | bytes 40
  4.6 47.8 %collective-permute-start = (f32[128,4096]{1,0:T(8,128)}, f32[128,4096]{1,0:T(8,128)}, u32[]{:S(2)}, u32[]{:S(2)}) collective-permute-start(f32[128,4096]{1,0:T(8,128)} %get-tuple-element.5.own), channel_id=1, source_target_pairs={{0,4},{4,8},{8,12},{12,16},{16,20},{20,24},{24,28},{28,0},{1,5},{5... | collective-permute-start | bytes 6291464 | tf_op jit(solution)/shard_map/ppermute | solution.py:18
  7.2 91.0 %collective-permute-start.1 = (f32[128,4096]{1,0:T(8,128)}, f32[128,4096]{1,0:T(8,128)}, u32[]{:S(2)}, u32[]{:S(2)}) collective-permute-start(f32[128,4096]{1,0:T(8,128)} %get-tuple-element.5.own), channel_id=1, source_target_pairs={{0,8},{4,12},{8,16},{12,20},{16,24},{20,28},{24,0},{28,4},{1,9},{5... | collective-permute-start | bytes 6291464 | tf_op jit(solution)/shard_map/ppermute | solution.py:18
  8.4 354.2 %collective-permute-start.2 = (f32[128,4096]{1,0:T(8,128)S(1)}, f32[128,4096]{1,0:T(8,128)}, u32[]{:S(2)}, u32[]{:S(2)}) collective-permute-start(f32[128,4096]{1,0:T(8,128)S(1)} %get-tuple-element.4.own), channel_id=1, source_target_pairs={{0,4},{4,8},{8,12},{12,16},{16,20},{20,24},{24,28},{28,0},{1,5},{5... | collective-permute-start | bytes 6291464 | tf_op jit(solution)/shard_map/ppermute | solution.py:18
  8.7 353.9 %collective-permute-start.3 = (f32[128,4096]{1,0:T(8,128)S(1)}, f32[128,4096]{1,0:T(8,128)}, u32[]{:S(2)}, u32[]{:S(2)}) collective-permute-start(f32[128,4096]{1,0:T(8,128)S(1)} %get-tuple-element.4.own), channel_id=1, source_target_pairs={{0,8},{4,12},{8,16},{12,20},{16,24},{20,28},{24,0},{28,4},{1,9},{5... | collective-permute-start | bytes 6291464 | tf_op jit(solution)/shard_map/ppermute | solution.py:18
  627.7 6.4 collective-permute-start.6
  632.1 6.7 %collective-permute-start.5 = (f32[228,128]{0,1:T(8,128)S(1)}, f32[228,128]{0,1:T(8,128)S(1)}, u32[]{:S(2)}, u32[]{:S(2)}) collective-permute-start(f32[228,128]{0,1:T(8,128)S(1)} %get-tuple-element.11), channel_id=1, source_target_pairs={{0,2},{1,3},{2,0},{3,1},{4,6},{5,7},{6,4},{7,5},{8,10},{9,11},{10,... | collective-permute-start | bytes 350216 | tf_op jit(solution)/shard_map/ppermute | solution.py:18
  632.1 6.7 %collective-permute-start.4 = (f32[228,128]{0,1:T(8,128)S(1)}, f32[228,128]{0,1:T(8,128)S(1)}, u32[]{:S(2)}, u32[]{:S(2)}) collective-permute-start(f32[228,128]{0,1:T(8,128)S(1)} %get-tuple-element.10), channel_id=1, source_target_pairs={{0,1},{1,2},{2,3},{3,0},{4,5},{5,6},{6,7},{7,4},{8,9},{9,10},{10,1... | collective-permute-start | bytes 350216 | tf_op jit(solution)/shard_map/ppermute | solution.py:18
  639.2 1.6 copy-start.2

commit v2 on v1

--- a/solution.py
+++ b/solution.py
@@ -8,9 +8,12 @@
 from jax.sharding import PartitionSpec as P
 
 FIELDS = 32768
-CHUNKS = 2
+FIRST = 4
 LANES = 128
 SUB = 8
+TRIPLE_COLS = 8
+PAIR_ROWS = 4
+UNROLL = 48
 
 
 def shifted(shard, axis, by):
@@ -60,31 +63,33 @@
     def triple_block(index, carry):
         row = (index // (rows // SUB)) * SUB
         col = (index % (rows // SUB)) * SUB
+        for half in range(0, SUB, TRIPLE_COLS):
 
-        def step(k, accs):
-            at = k * LANES
-            lead = tile(first, row, at)
-            tail = tile(last, col, at)
-            points = [piv[m, :, pl.ds(pl.multiple_of(at, LANES), LANES)] for m in range(count)]
-            new = []
-            for j in range(SUB):
-                both = jnp.minimum(lead, jnp.broadcast_to(tail[j : j + 1], (SUB, LANES)))
-                new.append(accs[j * (count + 1)] + both)
-                for m in range(count):
-                    new.append(accs[j * (count + 1) + 1 + m] + jnp.minimum(both, points[m]))
-            return tuple(new)
+            def step(k, accs, half=half):
+                at = k * LANES
+                lead = tile(first, row, at)
+                tail = tile(last, col, at)
+                points = [piv[m, :, pl.ds(pl.multiple_of(at, LANES), LANES)] for m in range(count)]
+                new = []
+                for j in range(TRIPLE_COLS):
+                    end = tail[half + j : half + j + 1]
+                    both = jnp.minimum(lead, jnp.broadcast_to(end, (SUB, LANES)))
+                    new.append(accs[j * (count + 1)] + both)
+                    for m in range(count):
+                        new.append(accs[j * (count + 1) + 1 + m] + jnp.minimum(both, points[m]))
+                return tuple(new)
 
-        zero = jnp.zeros((SUB, LANES), jnp.float32)
-        accs = lax.fori_loop(0, steps, step, (zero,) * (SUB * (count + 1)), unroll=unroll)
-        store(1, row, col, accs[0 :: count + 1])
-        for m in range(count):
-            store(3 + m, row, col, accs[1 + m :: count + 1])
+            zero = jnp.zeros((SUB, LANES), jnp.float32)
+            accs = lax.fori_loop(0, steps, step, (zero,) * (TRIPLE_COLS * (count + 1)), unroll=unroll)
+            store(1, row, col + half, accs[0 :: count + 1])
+            for m in range(count):
+                store(3 + m, row, col + half, accs[1 + m :: count + 1])
         return carry
 
     lax.fori_loop(0, (rows // SUB) ** 2, triple_block, 0)
 
     def pair_table(table, left, right):
-        group = 4 if rows % (4 * SUB) == 0 else 1
+        group = PAIR_ROWS if rows % (PAIR_ROWS * SUB) == 0 else 1
 
         def pair_block(index, carry):
             row = (index // (rows // SUB)) * SUB * group
@@ -120,7 +125,7 @@
     hbm = pl.BlockSpec(memory_space=pl.ANY)
     pairs = (3 + count) * rows * rows * width
     return pl.pallas_call(
-        functools.partial(table_kernel, 2),
+        functools.partial(table_kernel, min(UNROLL, width // LANES)),
         out_shape=jax.ShapeDtypeStruct((3 + count, rows, rows), jnp.float32),
         in_specs=[smem, smem, hbm, hbm, hbm],
         out_specs=pl.BlockSpec(memory_space=pltpu.VMEM),
@@ -143,11 +148,11 @@
     count_piv = pivots.shape[1]
     row_count = width // n
     chosen = pivots[0]
-    chunks = CHUNKS if fields % (CHUNKS * LANES) == 0 else 1
-    span = fields // chunks
+    cut = max(fields // (FIRST * LANES), 1) * LANES
+    spans = ((0, cut), (cut, fields)) if cut < fields else ((0, fields),)
     tables = None
-    for k in range(chunks):
-        own = profiles[:, k * span : (k + 1) * span]
+    for begin, end in spans:
+        own = profiles[:, begin:end]
         near = shifted(own, "vec", stride)
         far = shifted(own, "vec", 2 * stride)
         part = partial_tables(roles[0], chosen, own, near, far)

time: 641 us -> 526 us (0.82)
  Pallas kernels: 528 us -> 372 us
  waiting for transfers between devices: 94.4 us -> 135 us
    pallas_call x2, Pallas kernels: 528 us -> 372 us  [partial_tables(): pl.pallas_call(functools.partial(table_kernel, min(UNROLL, width // LANES...]
    ppermute x7, waiting for transfers between devices: 94.4 us -> 135 us  [shifted(): lax.ppermute(shard, axis, [(i, (i + by) % peers) for i in range(peers)])]
  transfers between devices with their start and end apart: 7 -> 7, of which waited for: 4 -> 5; matrix products, arithmetic and copies ran while one was open for 0% -> 0% of each run, Pallas kernels for 41% -> 18%
where the time goes in v2:
time: 526 us
  Pallas kernels  372 us (71%)
  waiting for transfers between devices  135 us (26%)
  starting transfers between devices  10.9 us (2%)
  local copies, waits for them, and re-layouts  7.21 us (1%)
    pallas_call x2, Pallas kernels, partial_tables(): pl.pallas_call(functools.partial(table_kernel, min(UNROLL, width // LANES...  372 us
    ppermute x7, waiting for transfers between devices, shifted(): lax.ppermute(shard, axis, [(i, (i + by) % peers) for i in range(peers)])  135 us
    ppermute x7, starting transfers between devices, shifted(): lax.ppermute(shard, axis, [(i, (i + by) % peers) for i in range(peers)])  10.9 us
  transfers between devices with their start and end apart: 7, of which 5 were waited for; matrix products, arithmetic and copies ran while one was open for 0% of the time, Pallas kernels for 18%

profile of v2, /device:TPU:1, one launch (start us, length us, event | category | flops | bytes accessed | tf_op | source)
XLA Modules:
  0.0 526.1 jit_solution(4668472139943322207)
XLA Ops:
  0.6 2.1 slice.36.own
  2.8 2.6 collective-permute-start.2
  5.4 1.2 collective-permute-start.3
  6.6 2.3 slice.35.own
  9.0 0.3 collective-permute-start
  9.3 1.2 collective-permute-start.1
  10.5 119.1 %collective-permute-done.near = f32[128,2048]{1,0:T(8,128)} collective-permute-done((f32[128,2048]{1,0:T(8,128)}, f32[128,2048]{1,0:T(8,128)}, u32[]{:S(2)}, u32[]{:S(2)}) %collective-permute-start) | collective-permute-done | bytes 1048608 | tf_op jit(solution)/shard_map/ppermute | solution.py:21
  129.6 12.1 %collective-permute-done.1.far = f32[128,2048]{1,0:T(8,128)} collective-permute-done((f32[128,2048]{1,0:T(8,128)}, f32[128,2048]{1,0:T(8,128)}, u32[]{:S(2)}, u32[]{:S(2)}) %collective-permute-start.1) | collective-permute-done | bytes 1048608 | tf_op jit(solution)/shard_map/ppermute | solution.py:21
  141.7 97.3 %shard_map.50 = f32[7,128,128]{2,1,0:T(8,128)S(1)} custom-call(s32[3]{0:T(128)S(1)} %bitcast.27, s32[4]{0:T(128)S(1)} %bitcast.29, f32[128,2048]{1,0:T(8,128)} %slice.35.own, f32[128,2048]{1,0:T(8,128)} %collective-permute-done.near, f32[128,2048]{1,0:T(8,128)} %collective-permute-done.1.far), custom_call_target="tpu_custom_call" | custom-call | flops 469762048 | bytes 3145728 | tf_op jit(solution)/shard_map/pallas_call | solution.py:127
  239.0 274.3 %shard_map.51 = f32[7,128,128]{2,1,0:T(8,128)S(1)} custom-call(s32[3]{0:T(128)S(1)} %bitcast.28, s32[4]{0:T(128)S(1)} %bitcast.30, f32[128,6144]{1,0:T(8,128)S(1)} %slice.36.own, f32[128,6144]{1,0:T(8,128)} %collective-permute-done.2.near, f32[128,6144]{1,0:T(8,128)} %collective-permute-done.3.far), custom_call_target="tpu_custom_call" | custom-call | flops 1409286144 | bytes 9437184 | tf_op jit(solution)/shard_map/pallas_call | solution.py:127
  513.5 0.1 copy.15
  513.6 0.1 copy.17
  513.8 0.6 gather_fusion
  514.4 0.1 copy.14
  514.6 2.1 collective-permute-start.4
  516.7 2.3 collective-permute-start.5
  519.0 1.1 collective-permute-start.6
  520.2 1.0 collective-permute-done.4
  521.2 2.8 collective-permute-done.5
  524.0 0.1 collective-permute-done.6
  524.4 0.1 copy.23
  524.7 0.6 gather_fusion.1
  525.4 0.1 multiply_bitcast_fusion
  525.5 0.7 copy.24
  (27 shorter events, 1.0 us)
Async XLA Ops:
  0.6 9.9 %copy-start.1 = (s32[1,4]{1,0:T(1,128)S(1)}, s32[1,4]{1,0:T(1,128)}, u32[]{:S(2)}) copy-start(s32[1,4]{1,0:T(1,128)} %param.4) | copy-start | bytes 52
  0.6 141.1 %copy-start = (s32[1,3]{1,0:T(1,128)S(1)}, s32[1,3]{1,0:T(1,128)}, u32[]{:S(2)}) copy-start(s32[1,3]{1,0:T(1,128)} %param.5) | copy-start | bytes 40
  2.8 236.2 %collective-permute-start.2 = (f32[128,6144]{1,0:T(8,128)S(1)}, f32[128,6144]{1,0:T(8,128)}, u32[]{:S(2)}, u32[]{:S(2)}) collective-permute-start(f32[128,6144]{1,0:T(8,128)S(1)} %slice.36.own), channel_id=1, source_target_pairs={{0,4},{4,8},{8,12},{12,16},{16,20},{20,24},{24,28},{28,0},{1,5},{5... | collective-permute-start | bytes 9437192 | tf_op jit(solution)/shard_map/ppermute | solution.py:21
  5.4 233.6 %collective-permute-start.3 = (f32[128,6144]{1,0:T(8,128)S(1)}, f32[128,6144]{1,0:T(8,128)}, u32[]{:S(2)}, u32[]{:S(2)}) collective-permute-start(f32[128,6144]{1,0:T(8,128)S(1)} %slice.36.own), channel_id=1, source_target_pairs={{0,8},{4,12},{8,16},{12,20},{16,24},{20,28},{24,0},{28,4},{1,9},{5... | collective-permute-start | bytes 9437192 | tf_op jit(solution)/shard_map/ppermute | solution.py:21
  9.0 120.7 %collective-permute-start = (f32[128,2048]{1,0:T(8,128)}, f32[128,2048]{1,0:T(8,128)}, u32[]{:S(2)}, u32[]{:S(2)}) collective-permute-start(f32[128,2048]{1,0:T(8,128)} %slice.35.own), channel_id=1, source_target_pairs={{0,4},{4,8},{8,12},{12,16},{16,20},{20,24},{24,28},{28,0},{1,5},{5... | collective-permute-start | bytes 3145736 | tf_op jit(solution)/shard_map/ppermute | solution.py:21
  9.3 132.4 %collective-permute-start.1 = (f32[128,2048]{1,0:T(8,128)}, f32[128,2048]{1,0:T(8,128)}, u32[]{:S(2)}, u32[]{:S(2)}) collective-permute-start(f32[128,2048]{1,0:T(8,128)} %slice.35.own), channel_id=1, source_target_pairs={{0,8},{4,12},{8,16},{12,20},{16,24},{20,28},{24,0},{28,4},{1,9},{5... | collective-permute-start | bytes 3145736 | tf_op jit(solution)/shard_map/ppermute | solution.py:21
  514.6 6.6 %collective-permute-start.4 = (f32[228,128]{0,1:T(8,128)S(1)}, f32[228,128]{0,1:T(8,128)S(1)}, u32[]{:S(2)}, u32[]{:S(2)}) collective-permute-start(f32[228,128]{0,1:T(8,128)S(1)} %get-tuple-element.8), channel_id=1, source_target_pairs={{0,1},{1,2},{2,3},{3,0},{4,5},{5,6},{6,7},{7,4},{8,9},{9,10},{10,1... | collective-permute-start | bytes 350216 | tf_op jit(solution)/shard_map/ppermute | solution.py:21
  516.7 7.3 %collective-permute-start.5 = (f32[228,128]{0,1:T(8,128)S(1)}, f32[228,128]{0,1:T(8,128)S(1)}, u32[]{:S(2)}, u32[]{:S(2)}) collective-permute-start(f32[228,128]{0,1:T(8,128)S(1)} %get-tuple-element.9), channel_id=1, source_target_pairs={{0,2},{1,3},{2,0},{3,1},{4,6},{5,7},{6,4},{7,5},{8,10},{9,11},{10,... | collective-permute-start | bytes 350216 | tf_op jit(solution)/shard_map/ppermute | solution.py:21
  519.0 5.1 collective-permute-start.6
  524.6 1.5 copy-start.2

commit v3 on v2

--- a/solution.py
+++ b/solution.py
@@ -13,7 +13,7 @@
 SUB = 8
 TRIPLE_COLS = 8
 PAIR_ROWS = 4
-UNROLL = 48
+UNROLL = 16
 
 
 def shifted(shard, axis, by):
@@ -151,10 +151,14 @@
     cut = max(fields // (FIRST * LANES), 1) * LANES
     spans = ((0, cut), (cut, fields)) if cut < fields else ((0, fields),)
     tables = None
+    owned, arrived = [], []
     for begin, end in spans:
         own = profiles[:, begin:end]
-        near = shifted(own, "vec", stride)
-        far = shifted(own, "vec", 2 * stride)
+        if arrived:
+            own, *arrived[-1] = lax.optimization_barrier((own, *arrived[-1]))
+        arrived.append([shifted(own, "vec", stride), shifted(own, "vec", 2 * stride)])
+        owned.append(own)
+    for own, (near, far) in zip(owned, arrived):
         part = partial_tables(roles[0], chosen, own, near, far)
         tables = part if tables is None else tables + part
 

time: 526 us -> 411 us (0.78)
  waiting for transfers between devices: 135 us -> 43.7 us
  Pallas kernels: 372 us -> 345 us
    ppermute x7, waiting for transfers between devices: 135 us -> 43.7 us  [shifted(): lax.ppermute(shard, axis, [(i, (i + by) % peers) for i in range(peers)])]
    pallas_call x2, Pallas kernels: 372 us -> 345 us  [partial_tables(): pl.pallas_call(functools.partial(table_kernel, min(UNROLL, width // LANES...]
    unnamed x7 -> x19, local copies, waits for them, and re-layouts: 0.69 us -> 6.45 us
  transfers between devices with their start and end apart: 7 -> 7, of which waited for: 5 -> 5; matrix products, arithmetic and copies ran while one was open for 0% -> 1% of each run, Pallas kernels for 18% -> 23%
where the time goes in v3:
time: 411 us
  Pallas kernels  345 us (84%)
  waiting for transfers between devices  43.7 us (11%)
  local copies, waits for them, and re-layouts  11.9 us (3%)
  starting transfers between devices  8.75 us (2%)
    pallas_call x2, Pallas kernels, partial_tables(): pl.pallas_call(functools.partial(table_kernel, min(UNROLL, width // LANES...  345 us
    ppermute x7, waiting for transfers between devices, shifted(): lax.ppermute(shard, axis, [(i, (i + by) % peers) for i in range(peers)])  43.7 us
    ppermute x7, starting transfers between devices, shifted(): lax.ppermute(shard, axis, [(i, (i + by) % peers) for i in range(peers)])  8.75 us
  transfers between devices with their start and end apart: 7, of which 5 were waited for; matrix products, arithmetic and copies ran while one was open for 1% of the time, Pallas kernels for 23%

profile of v3, /device:TPU:1, one launch (start us, length us, event | category | flops | bytes accessed | tf_op | source)
XLA Modules:
  0.0 410.7 jit_solution(4315732903795956140)
XLA Ops:
  0.6 1.3 slice.35.own
  2.0 2.6 collective-permute-start
  4.6 1.2 collective-permute-start.1
  5.8 2.1 slice.36.own
  7.9 19.0 %collective-permute-done.near = f32[128,2048]{1,0:T(8,128)S(1)} collective-permute-done((f32[128,2048]{1,0:T(8,128)S(1)}, f32[128,2048]{1,0:T(8,128)S(1)}, u32[]{:S(2)}, u32[]{:S(2)}) %collective-permute-start) | collective-permute-done | bytes 1048608 | tf_op jit(solution)/shard_map/ppermute | solution.py:21
  27.0 1.0 copy-done.2
  28.0 11.7 %collective-permute-done.1.far = f32[128,2048]{1,0:T(8,128)S(1)} collective-permute-done((f32[128,2048]{1,0:T(8,128)S(1)}, f32[128,2048]{1,0:T(8,128)S(1)}, u32[]{:S(2)}, u32[]{:S(2)}) %collective-permute-start.1) | collective-permute-done | bytes 1048608 | tf_op jit(solution)/shard_map/ppermute | solution.py:21
  39.7 1.1 copy-done.4
  40.7 1.1 collective-permute-start.3
  41.8 1.2 copy-done.1
  43.1 1.2 copy-done.3
  44.3 1.2 copy-done.5
  45.5 95.7 %shard_map.50 = f32[7,128,128]{2,1,0:T(8,128)S(1)} custom-call(s32[3]{0:T(128)S(1)} %bitcast.27, s32[4]{0:T(128)S(1)} %bitcast.29, f32[128,2048]{1,0:T(8,128)S(1)} %copy-done.1, f32[128,2048]{1,0:T(8,128)S(1)} %copy-done.3, f32[128,2048]{1,0:T(8,128)S(1)} %copy-done.5), custom_call_target="tpu_custom_call" | custom-call | flops 469762048 | bytes 3145728 | tf_op jit(solution)/shard_map/pallas_call | solution.py:127
  141.2 3.7 collective-permute-done.3.far
  144.9 249.2 %shard_map.51 = f32[7,128,128]{2,1,0:T(8,128)S(1)} custom-call(s32[3]{0:T(128)S(1)} %bitcast.28, s32[4]{0:T(128)S(1)} %bitcast.30, f32[128,6144]{1,0:T(8,128)S(1)} %slice.36.own, f32[128,6144]{1,0:T(8,128)} %collective-permute-done.2.near, f32[128,6144]{1,0:T(8,128)} %collective-permute-done.3.far), custom_call_target="tpu_custom_call" | custom-call | flops 1409286144 | bytes 9437184 | tf_op jit(solution)/shard_map/pallas_call | solution.py:127
  394.2 0.6 gather_fusion
  394.8 0.1 copy.14
  395.1 0.1 copy.17
  395.4 3.4 collective-permute-start.6
  398.8 0.5 collective-permute-start.4
  399.3 2.8 collective-permute-done.6
  402.1 6.6 %collective-permute-done.5 = f32[228,128]{0,1:T(8,128)S(1)} collective-permute-done((f32[228,128]{0,1:T(8,128)S(1)}, f32[228,128]{0,1:T(8,128)S(1)}, u32[]{:S(2)}, u32[]{:S(2)}) %collective-permute-start.5) | collective-permute-done | bytes 116768 | tf_op jit(solution)/shard_map/ppermute | solution.py:21
  409.2 0.6 gather_fusion.1
  410.0 0.7 copy.24
  (39 shorter events, 1.3 us)
Async XLA Ops:
  1.9 37.7 %copy-start = (f32[128,2048]{1,0:T(8,128)}, f32[128,2048]{1,0:T(8,128)S(1)}, u32[]{:S(2)}) copy-start(f32[128,2048]{1,0:T(8,128)S(1)} %slice.35.own) | copy-start | bytes 3145732
  1.9 39.8 %copy-start.7 = (s32[1,4]{1,0:T(1,128)S(1)}, s32[1,4]{1,0:T(1,128)}, u32[]{:S(2)}) copy-start(s32[1,4]{1,0:T(1,128)} %param.4) | copy-start | bytes 52
  2.0 39.9 %copy-start.6 = (s32[1,3]{1,0:T(1,128)S(1)}, s32[1,3]{1,0:T(1,128)}, u32[]{:S(2)}) copy-start(s32[1,3]{1,0:T(1,128)} %param.5) | copy-start | bytes 40
  2.0 25.0 %collective-permute-start = (f32[128,2048]{1,0:T(8,128)S(1)}, f32[128,2048]{1,0:T(8,128)S(1)}, u32[]{:S(2)}, u32[]{:S(2)}) collective-permute-start(f32[128,2048]{1,0:T(8,128)S(1)} %slice.35.own), channel_id=1, source_target_pairs={{0,4},{4,8},{8,12},{12,16},{16,20},{20,24},{24,28},{28,0},{1,5},{5... | collective-permute-start | bytes 3145736 | tf_op jit(solution)/shard_map/ppermute | solution.py:21
  4.6 35.1 %collective-permute-start.1 = (f32[128,2048]{1,0:T(8,128)S(1)}, f32[128,2048]{1,0:T(8,128)S(1)}, u32[]{:S(2)}, u32[]{:S(2)}) collective-permute-start(f32[128,2048]{1,0:T(8,128)S(1)} %slice.35.own), channel_id=1, source_target_pairs={{0,8},{4,12},{8,16},{12,20},{16,24},{20,28},{24,0},{28,4},{1,9},{5... | collective-permute-start | bytes 3145736 | tf_op jit(solution)/shard_map/ppermute | solution.py:21
  27.0 1.0 copy-start.2
  39.7 1.1 copy-start.4
  40.7 100.5 %collective-permute-start.2 = (f32[128,6144]{1,0:T(8,128)S(1)}, f32[128,6144]{1,0:T(8,128)}, u32[]{:S(2)}, u32[]{:S(2)}) collective-permute-start(f32[128,6144]{1,0:T(8,128)S(1)} %slice.36.own), channel_id=1, source_target_pairs={{0,4},{4,8},{8,12},{12,16},{16,20},{20,24},{24,28},{28,0},{1,5},{5... | collective-permute-start | bytes 9437192 | tf_op jit(solution)/shard_map/ppermute | solution.py:21
  40.7 104.2 %collective-permute-start.3 = (f32[128,6144]{1,0:T(8,128)S(1)}, f32[128,6144]{1,0:T(8,128)}, u32[]{:S(2)}, u32[]{:S(2)}) collective-permute-start(f32[128,6144]{1,0:T(8,128)S(1)} %slice.36.own), channel_id=1, source_target_pairs={{0,8},{4,12},{8,16},{12,20},{16,24},{20,28},{24,0},{28,4},{1,9},{5... | collective-permute-start | bytes 9437192 | tf_op jit(solution)/shard_map/ppermute | solution.py:21
  41.8 1.2 copy-start.1
  43.1 1.2 copy-start.3
  44.3 1.2 copy-start.5
  395.4 6.7 %collective-permute-start.6 = (f32[228,128]{0,1:T(8,128)S(1)}, f32[228,128]{0,1:T(8,128)S(1)}, u32[]{:S(2)}, u32[]{:S(2)}) collective-permute-start(f32[228,128]{0,1:T(8,128)S(1)} %get-tuple-element.16), channel_id=1, source_target_pairs={{0,3},{1,0},{2,1},{3,2},{4,7},{5,4},{6,5},{7,6},{8,11},{9,8},{10,9... | collective-permute-start | bytes 350216 | tf_op jit(solution)/shard_map/ppermute | solution.py:21
  398.8 9.9 %collective-permute-start.5 = (f32[228,128]{0,1:T(8,128)S(1)}, f32[228,128]{0,1:T(8,128)S(1)}, u32[]{:S(2)}, u32[]{:S(2)}) collective-permute-start(f32[228,128]{0,1:T(8,128)S(1)} %get-tuple-element.15), channel_id=1, source_target_pairs={{0,2},{1,3},{2,0},{3,1},{4,6},{5,7},{6,4},{7,5},{8,10},{9,11},{10,... | collective-permute-start | bytes 350216 | tf_op jit(solution)/shard_map/ppermute | solution.py:21
  398.8 9.9 %collective-permute-start.4 = (f32[228,128]{0,1:T(8,128)S(1)}, f32[228,128]{0,1:T(8,128)S(1)}, u32[]{:S(2)}, u32[]{:S(2)}) collective-permute-start(f32[228,128]{0,1:T(8,128)S(1)} %get-tuple-element.14), channel_id=1, source_target_pairs={{0,1},{1,2},{2,3},{3,0},{4,5},{5,6},{6,7},{7,4},{8,9},{9,10},{10,1... | collective-permute-start | bytes 350216 | tf_op jit(solution)/shard_map/ppermute | solution.py:21
  409.1 1.6 copy-start.8

commit v4 on v3

--- a/solution.py
+++ b/solution.py
@@ -13,7 +13,7 @@
 SUB = 8
 TRIPLE_COLS = 8
 PAIR_ROWS = 4
-UNROLL = 16
+UNROLL = 24
 
 
 def shifted(shard, axis, by):

time: 411 us -> 405 us (0.985)
  Pallas kernels: 345 us -> 339 us
    pallas_call x2, Pallas kernels: 345 us -> 339 us  [partial_tables(): pl.pallas_call(functools.partial(table_kernel, min(UNROLL, width // LANES...]
  transfers between devices with their start and end apart: 7 -> 7, of which waited for: 5 -> 5; matrix products, arithmetic and copies ran while one was open for 1% -> 1% of each run, Pallas kernels for 23% -> 24%
where the time goes in v4:
time: 405 us
  Pallas kernels  339 us (84%)
  waiting for transfers between devices  43.7 us (11%)
  local copies, waits for them, and re-layouts  11.9 us (3%)
  starting transfers between devices  8.75 us (2%)
    pallas_call x2, Pallas kernels, partial_tables(): pl.pallas_call(functools.partial(table_kernel, min(UNROLL, width // LANES...  339 us
    ppermute x7, waiting for transfers between devices, shifted(): lax.ppermute(shard, axis, [(i, (i + by) % peers) for i in range(peers)])  43.7 us
    ppermute x7, starting transfers between devices, shifted(): lax.ppermute(shard, axis, [(i, (i + by) % peers) for i in range(peers)])  8.75 us
  transfers between devices with their start and end apart: 7, of which 5 were waited for; matrix products, arithmetic and copies ran while one was open for 1% of the time, Pallas kernels for 24%

profile of v4, /device:TPU:1, one launch (start us, length us, event | category | flops | bytes accessed | tf_op | source)
XLA Modules:
  0.0 404.7 jit_solution(2585564704817612290)
XLA Ops:
  0.6 1.3 slice.35.own
  2.0 2.6 collective-permute-start
  4.6 1.2 collective-permute-start.1
  5.8 2.1 slice.36.own
  7.9 19.0 %collective-permute-done.near = f32[128,2048]{1,0:T(8,128)S(1)} collective-permute-done((f32[128,2048]{1,0:T(8,128)S(1)}, f32[128,2048]{1,0:T(8,128)S(1)}, u32[]{:S(2)}, u32[]{:S(2)}) %collective-permute-start) | collective-permute-done | bytes 1048608 | tf_op jit(solution)/shard_map/ppermute | solution.py:21
  27.0 1.0 copy-done.2
  28.0 11.7 %collective-permute-done.1.far = f32[128,2048]{1,0:T(8,128)S(1)} collective-permute-done((f32[128,2048]{1,0:T(8,128)S(1)}, f32[128,2048]{1,0:T(8,128)S(1)}, u32[]{:S(2)}, u32[]{:S(2)}) %collective-permute-start.1) | collective-permute-done | bytes 1048608 | tf_op jit(solution)/shard_map/ppermute | solution.py:21
  39.7 1.1 copy-done.4
  40.7 1.1 collective-permute-start.3
  41.8 1.2 copy-done.1
  43.1 1.2 copy-done.3
  44.3 1.2 copy-done.5
  45.5 95.7 %shard_map.50 = f32[7,128,128]{2,1,0:T(8,128)S(1)} custom-call(s32[3]{0:T(128)S(1)} %bitcast.27, s32[4]{0:T(128)S(1)} %bitcast.29, f32[128,2048]{1,0:T(8,128)S(1)} %copy-done.1, f32[128,2048]{1,0:T(8,128)S(1)} %copy-done.3, f32[128,2048]{1,0:T(8,128)S(1)} %copy-done.5), custom_call_target="tpu_custom_call" | custom-call | flops 469762048 | bytes 3145728 | tf_op jit(solution)/shard_map/pallas_call | solution.py:127
  141.2 3.7 collective-permute-done.3.far
  144.9 243.3 %shard_map.51 = f32[7,128,128]{2,1,0:T(8,128)S(1)} custom-call(s32[3]{0:T(128)S(1)} %bitcast.28, s32[4]{0:T(128)S(1)} %bitcast.30, f32[128,6144]{1,0:T(8,128)S(1)} %slice.36.own, f32[128,6144]{1,0:T(8,128)} %collective-permute-done.2.near, f32[128,6144]{1,0:T(8,128)} %collective-permute-done.3.far), custom_call_target="tpu_custom_call" | custom-call | flops 1409286144 | bytes 9437184 | tf_op jit(solution)/shard_map/pallas_call | solution.py:127
  388.3 0.6 gather_fusion
  388.9 0.1 copy.14
  389.0 0.1 copy.15
  389.5 3.4 collective-permute-start.6
  392.8 0.5 collective-permute-start.4
  393.4 2.8 collective-permute-done.6
  396.1 6.6 %collective-permute-done.5 = f32[228,128]{0,1:T(8,128)S(1)} collective-permute-done((f32[228,128]{0,1:T(8,128)S(1)}, f32[228,128]{0,1:T(8,128)S(1)}, u32[]{:S(2)}, u32[]{:S(2)}) %collective-permute-start.5) | collective-permute-done | bytes 116768 | tf_op jit(solution)/shard_map/ppermute | solution.py:21
  403.3 0.6 gather_fusion.1
  404.0 0.7 copy.24
  (39 shorter events, 1.3 us)
Async XLA Ops:
  1.9 37.7 %copy-start = (f32[128,2048]{1,0:T(8,128)}, f32[128,2048]{1,0:T(8,128)S(1)}, u32[]{:S(2)}) copy-start(f32[128,2048]{1,0:T(8,128)S(1)} %slice.35.own) | copy-start | bytes 3145732
  1.9 39.8 %copy-start.7 = (s32[1,4]{1,0:T(1,128)S(1)}, s32[1,4]{1,0:T(1,128)}, u32[]{:S(2)}) copy-start(s32[1,4]{1,0:T(1,128)} %param.4) | copy-start | bytes 52
  2.0 39.9 %copy-start.6 = (s32[1,3]{1,0:T(1,128)S(1)}, s32[1,3]{1,0:T(1,128)}, u32[]{:S(2)}) copy-start(s32[1,3]{1,0:T(1,128)} %param.5) | copy-start | bytes 40
  2.0 25.0 %collective-permute-start = (f32[128,2048]{1,0:T(8,128)S(1)}, f32[128,2048]{1,0:T(8,128)S(1)}, u32[]{:S(2)}, u32[]{:S(2)}) collective-permute-start(f32[128,2048]{1,0:T(8,128)S(1)} %slice.35.own), channel_id=1, source_target_pairs={{0,4},{4,8},{8,12},{12,16},{16,20},{20,24},{24,28},{28,0},{1,5},{5... | collective-permute-start | bytes 3145736 | tf_op jit(solution)/shard_map/ppermute | solution.py:21
  4.6 35.1 %collective-permute-start.1 = (f32[128,2048]{1,0:T(8,128)S(1)}, f32[128,2048]{1,0:T(8,128)S(1)}, u32[]{:S(2)}, u32[]{:S(2)}) collective-permute-start(f32[128,2048]{1,0:T(8,128)S(1)} %slice.35.own), channel_id=1, source_target_pairs={{0,8},{4,12},{8,16},{12,20},{16,24},{20,28},{24,0},{28,4},{1,9},{5... | collective-permute-start | bytes 3145736 | tf_op jit(solution)/shard_map/ppermute | solution.py:21
  27.0 1.0 copy-start.2
  39.7 1.1 copy-start.4
  40.7 100.5 %collective-permute-start.2 = (f32[128,6144]{1,0:T(8,128)S(1)}, f32[128,6144]{1,0:T(8,128)}, u32[]{:S(2)}, u32[]{:S(2)}) collective-permute-start(f32[128,6144]{1,0:T(8,128)S(1)} %slice.36.own), channel_id=1, source_target_pairs={{0,4},{4,8},{8,12},{12,16},{16,20},{20,24},{24,28},{28,0},{1,5},{5... | collective-permute-start | bytes 9437192 | tf_op jit(solution)/shard_map/ppermute | solution.py:21
  40.7 104.2 %collective-permute-start.3 = (f32[128,6144]{1,0:T(8,128)S(1)}, f32[128,6144]{1,0:T(8,128)}, u32[]{:S(2)}, u32[]{:S(2)}) collective-permute-start(f32[128,6144]{1,0:T(8,128)S(1)} %slice.36.own), channel_id=1, source_target_pairs={{0,8},{4,12},{8,16},{12,20},{16,24},{20,28},{24,0},{28,4},{1,9},{5... | collective-permute-start | bytes 9437192 | tf_op jit(solution)/shard_map/ppermute | solution.py:21
  41.8 1.2 copy-start.1
  43.1 1.2 copy-start.3
  44.3 1.2 copy-start.5
  389.5 6.7 %collective-permute-start.6 = (f32[228,128]{0,1:T(8,128)S(1)}, f32[228,128]{0,1:T(8,128)S(1)}, u32[]{:S(2)}, u32[]{:S(2)}) collective-permute-start(f32[228,128]{0,1:T(8,128)S(1)} %get-tuple-element.16), channel_id=1, source_target_pairs={{0,3},{1,0},{2,1},{3,2},{4,7},{5,4},{6,5},{7,6},{8,11},{9,8},{10,9... | collective-permute-start | bytes 350216 | tf_op jit(solution)/shard_map/ppermute | solution.py:21
  392.8 9.9 %collective-permute-start.5 = (f32[228,128]{0,1:T(8,128)S(1)}, f32[228,128]{0,1:T(8,128)S(1)}, u32[]{:S(2)}, u32[]{:S(2)}) collective-permute-start(f32[228,128]{0,1:T(8,128)S(1)} %get-tuple-element.15), channel_id=1, source_target_pairs={{0,2},{1,3},{2,0},{3,1},{4,6},{5,7},{6,4},{7,5},{8,10},{9,11},{10,... | collective-permute-start | bytes 350216 | tf_op jit(solution)/shard_map/ppermute | solution.py:21
  392.8 9.9 %collective-permute-start.4 = (f32[228,128]{0,1:T(8,128)S(1)}, f32[228,128]{0,1:T(8,128)S(1)}, u32[]{:S(2)}, u32[]{:S(2)}) collective-permute-start(f32[228,128]{0,1:T(8,128)S(1)} %get-tuple-element.14), channel_id=1, source_target_pairs={{0,1},{1,2},{2,3},{3,0},{4,5},{5,6},{6,7},{7,4},{8,9},{9,10},{10,1... | collective-permute-start | bytes 350216 | tf_op jit(solution)/shard_map/ppermute | solution.py:21
  403.1 1.6 copy-start.8
